TPU v7x, 32 devices: a whole 2x2x4 slice. The times are simulated.
32 devices in a mesh: row: 16 (over z, x, core), col: 2 (over y).
Axes of the slice: x: 2, y: 2, z: 4, core: 2. Of those that a mesh axis runs over, the one named last changes fastest.
Arguments:
- solution: float32 [8, 1024, 2048], P(None, 'row', 'col'), may hold values from -1 to 1, as said below
- search: float32 [8, 1024, 2048], P(None, 'row', 'col'), may hold values from -1 to 1, as said below
- basis: float32 [8, 1024, 2048], P(None, 'row', 'col'), may hold values from -1 to 1, as said below
- resid_a: float32 [1024, 2048], P('row', 'col'), may hold values from -1 to 1, as said below
- resid_b: float32 [1024, 2048], P('row', 'col'), may hold values from -1 to 1, as said below
- scalars: float32 [3], replicated, may hold values from 0.5 to 2
- profile_a: float32 [8, 512], replicated, may hold values from -0.25 to 0.25
- profile_b: float32 [8, 512], replicated, may hold values from -0.25 to 0.25
- source_mask: int32 [1024, 2048], P('row', 'col'), may hold values 0 or 1
- weight_code: int32 [1024, 2048], P('row', 'col'), may hold values from 0 to 7
- roll_code: int32 [1024, 2048], P('row', 'col'), may hold values from 0 to 2
Outputs:
- next_solution: float32 [8, 1024, 2048], P(None, 'row', 'col')
- next_search: float32 [8, 1024, 2048], P(None, 'row', 'col')
- next_basis: float32 [8, 1024, 2048], P(None, 'row', 'col')
- next_resid_a: float32 [1024, 2048], P('row', 'col')
- next_resid_b: float32 [1024, 2048], P('row', 'col')
Inputs may be any that keep to these rules, and one draw needn't show every extreme that they name: `solution`: the whole array has Euclidean norm 1. `search`: the whole array has Euclidean norm 1. `basis`: the whole array has Euclidean norm 1. Euclidean norm sqrt(1/2), so that resid_a and resid_b together have norm 1. Euclidean norm sqrt(1/2), so that resid_a and resid_b together have norm 1.
All inputs are finite; a program needn't handle non-finite values. No bound on the sum of `source_mask` on one device may be relied on, other than what follows from the above.
Results may differ from a plain program's by a relative error of at most 0.000078.
Values sent between devices are 32-bit elements; how exact they have to be, the bound alone decides.
No kernel may reach another device: no remote copies, remote signals or barrier semaphores. Data moves between devices by JAX's collectives and lax.ppermute only.
A program may use at most 128 MiB of HBM per device.

v0:
```python
import math

import jax
import jax.numpy as jnp
from jax import lax
from jax.sharding import PartitionSpec as P

precise = lax.Precision.HIGHEST
epsilon = 1e-12


def shifted(block, axis, distance):
    devices = range(lax.axis_size(axis))
    route = [(i - distance, i) for i in devices if i - distance in devices]
    return lax.ppermute(block, axis, route)


def roll_weights(weight_code, roll_code):
    base = 1.0 / (1.0 + 0.25 * weight_code.astype(jnp.float32))
    return (
        base * (roll_code != 2).astype(jnp.float32),
        base * (roll_code != 1).astype(jnp.float32),
    )


def band_table(profile, width, count):
    maps_count, length = profile.shape
    period = (count + 1) * width
    padded = jnp.pad(profile, ((0, 0), (0, period - length)))
    tiled = jnp.tile(padded, (1, width))[:, : width * (period - 1)]
    skewed = tiled.reshape(maps_count, width, period - 1)[:, :, : count * width]
    return jnp.transpose(skewed.reshape(maps_count, width, count, width), (2, 0, 1, 3))


def cols_forward(padded, table, first, count):
    width = table.shape[2]
    maps_count, rows_here, extent = padded.shape
    blocks = padded.reshape(maps_count, rows_here, extent // width, width)
    total = jnp.zeros((rows_here, count, width), jnp.float32)
    for lead in range(table.shape[0]):
        picked = blocks[:, :, first - lead : first - lead + count]
        total = total + jnp.einsum("krns,ksc->rnc", picked, table[lead], precision=precise)
    return total.reshape(rows_here, count * width)


def cols_adjoint(padded, table, count):
    width = table.shape[2]
    rows_here, extent = padded.shape
    blocks = padded.reshape(rows_here, extent // width, width)
    total = jnp.zeros((table.shape[1], rows_here, count, width), jnp.float32)
    for lead in range(table.shape[0]):
        picked = blocks[:, lead : lead + count]
        total = total + jnp.einsum("rnj,kcj->krnc", picked, table[lead], precision=precise)
    return total.reshape(table.shape[1], rows_here, count * width)


def rows_forward(padded, table, first, count):
    width = table.shape[2]
    maps_count, extent, cols_here = padded.shape
    blocks = padded.reshape(maps_count, extent // width, width, cols_here)
    total = jnp.zeros((count, width, cols_here), jnp.float32)
    for lead in range(table.shape[0]):
        picked = blocks[:, first - lead : first - lead + count]
        total = total + jnp.einsum("knsc,ksr->nrc", picked, table[lead], precision=precise)
    return total.reshape(count * width, cols_here)


def rows_adjoint(padded, table, count):
    width = table.shape[2]
    extent, cols_here = padded.shape
    blocks = padded.reshape(extent // width, width, cols_here)
    total = jnp.zeros((table.shape[1], count, width, cols_here), jnp.float32)
    for lead in range(table.shape[0]):
        picked = blocks[lead : lead + count]
        total = total + jnp.einsum("njc,krj->knrc", picked, table[lead], precision=precise)
    return total.reshape(table.shape[1], count * width, cols_here)


def forward(source, weight_a, weight_b, table_a, table_b, length):
    rows_here = source.shape[1]
    cols_here = source.shape[2]
    col_depth = -(-(length - 1) // cols_here)
    row_depth = -(-(length - 1) // rows_here)
    col_width = table_a.shape[2]
    row_width = table_b.shape[2]
    col_lead = table_a.shape[0] - 1
    row_lead = table_b.shape[0] - 1
    pieces = [shifted(source, "col", level + 1) for level in range(col_depth)]
    extended = jnp.concatenate(pieces[::-1] + [source], axis=2)
    padded = jnp.pad(extended, ((0, 0), (0, 0), (col_lead * col_width, 0)))
    image_a = cols_forward(
        padded, table_a, col_lead + col_depth * cols_here // col_width, cols_here // col_width
    )
    padded = jnp.pad(source, ((0, 0), (row_lead * row_width, row_depth * rows_here), (0, 0)))
    partial_rows = rows_forward(padded, table_b, row_lead, (row_depth + 1) * rows_here // row_width)
    image_b = partial_rows[:rows_here]
    for level in range(1, row_depth + 1):
        block = partial_rows[level * rows_here : (level + 1) * rows_here]
        image_b = image_b + shifted(block, "row", level)
    return (weight_a * image_a, weight_b * image_b)


def adjoint(first, second, masked, weight_a, weight_b, table_a, table_b, length):
    rows_here, cols_here = first.shape
    col_depth = -(-(length - 1) // cols_here)
    row_depth = -(-(length - 1) // rows_here)
    col_width = table_a.shape[2]
    row_width = table_b.shape[2]
    col_lead = table_a.shape[0] - 1
    row_lead = table_b.shape[0] - 1
    weighted_a = weight_a * first
    weighted_b = weight_b * second
    pieces = [shifted(weighted_a, "col", -(level + 1)) for level in range(col_depth)]
    extended = jnp.concatenate([weighted_a] + pieces, axis=1)
    padded = jnp.pad(extended, ((0, 0), (0, col_lead * col_width)))
    grad_a = cols_adjoint(padded, table_a, cols_here // col_width)
    pieces = [shifted(weighted_b, "row", -(level + 1)) for level in range(row_depth)]
    extended = jnp.concatenate([weighted_b] + pieces, axis=0)
    padded = jnp.pad(extended, ((0, row_lead * row_width), (0, 0)))
    grad_b = rows_adjoint(padded, table_b, rows_here // row_width)
    return masked[None] * (grad_a + grad_b)


def body(
    solution,
    search,
    basis,
    resid_a,
    resid_b,
    scalars,
    profile_a,
    profile_b,
    source_mask,
    weight_code,
    roll_code,
):
    alpha = scalars[0]
    phibar = scalars[1]
    rhobar = scalars[2]
    length = profile_a.shape[1]
    rows_here, cols_here = resid_a.shape
    col_width = math.gcd(128, cols_here)
    row_width = math.gcd(128, rows_here)
    table_a = band_table(profile_a, col_width, (length + col_width - 2) // col_width + 1)
    table_b = band_table(profile_b, row_width, (length + row_width - 2) // row_width + 1)
    weight_a, weight_b = roll_weights(weight_code, roll_code)
    masked = source_mask.astype(jnp.float32)
    image_a, image_b = forward(basis * masked[None], weight_a, weight_b, table_a, table_b, length)
    raw_a = image_a - alpha * resid_a
    raw_b = image_b - alpha * resid_b
    beta = jnp.sqrt(
        lax.psum(jnp.sum(raw_a * raw_a) + jnp.sum(raw_b * raw_b), ("row", "col")) + epsilon
    )
    next_resid_a = raw_a / beta
    next_resid_b = raw_b / beta
    raw_v = (
        adjoint(next_resid_a, next_resid_b, masked, weight_a, weight_b, table_a, table_b, length)
        - beta * basis
    )
    alpha_next = jnp.sqrt(lax.psum(jnp.sum(raw_v * raw_v), ("row", "col")) + epsilon)
    next_basis = raw_v / alpha_next
    rho_total = jnp.sqrt(rhobar * rhobar + beta * beta)
    cosine = rhobar / rho_total
    sine = beta / rho_total
    theta = sine * alpha_next
    phi_value = cosine * phibar
    next_solution = solution + phi_value / rho_total * search
    next_search = next_basis - theta / rho_total * search
    return (next_solution, next_search, next_basis, next_resid_a, next_resid_b)


def solution(mesh):
    placed = (
        P(None, "row", "col"),
        P(None, "row", "col"),
        P(None, "row", "col"),
        P("row", "col"),
        P("row", "col"),
        P(),
        P(),
        P(),
        P("row", "col"),
        P("row", "col"),
        P("row", "col"),
    )
    return jax.shard_map(
        body,
        mesh=mesh,
        in_specs=placed,
        out_specs=(
            P(None, "row", "col"),
            P(None, "row", "col"),
            P(None, "row", "col"),
            P("row", "col"),
            P("row", "col"),
        ),
        check_vma=False,
    )
```

profile of v0, /device:TPU:12, one launch (start us, length us, event | category | flops | bytes accessed | tf_op | source)
XLA Modules:
  0.0 454.9 jit_solution(17948104784476371851)
XLA Ops:
  1.6 3.3 broadcast_multiply_fusion
  6.4 13.0 %pad.25 = f32[8,1088,1024]{2,1,0:T(8,128)} pad(f32[8,64,1024]{2,1,0:T(8,128)} %broadcast_multiply_fusion, f32[]{:T(128)} %constant.5.clone.1), padding=0_0x512_512x0_0 | pad | bytes 37748740 | tf_op jit(solution)/shard_map/jit(_pad)/pad | solution.py:94
  24.7 18.0 %fusion = f32[64,9,1024,1]{2,0,1,3:T(8,128)S(1)} fusion(f32[8,17,64,1024]{3,2,1,0:T(8,128)} %bitcast.329, f32[9,8,64,64]{2,3,1,0:T(8,128)S(1)} %bitcast.348), kind=kOutput, calls=%fused_computation | convolution fusion | flops 3623878656 | bytes 21495808 | tf_op jit(solution)/shard_map/knsc,ksr->nrc/dot_general | solution.py:64
  42.7 17.1 %fusion.10 = f32[64,9,1024,1]{2,0,1,3:T(8,128)S(1)} fusion(f32[8,17,64,1024]{3,2,1,0:T(8,128)} %bitcast.330, f32[9,8,64,64]{2,3,1,0:T(8,128)S(1)} %bitcast.349), kind=kOutput, calls=%fused_computation.10 | convolution fusion | flops 3623878656 | bytes 21495808 | tf_op jit(solution)/shard_map/knsc,ksr->nrc/dot_general | solution.py:64
  59.8 17.4 %fusion.12 = f32[64,9,1024,1]{2,0,1,3:T(8,128)S(1)} fusion(f32[8,17,64,1024]{3,2,1,0:T(8,128)} %bitcast.331, f32[9,8,64,64]{2,3,1,0:T(8,128)S(1)} %bitcast.350), kind=kOutput, calls=%fused_computation.12 | convolution fusion | flops 3623878656 | bytes 21495808 | tf_op jit(solution)/shard_map/knsc,ksr->nrc/dot_general | solution.py:64
  77.2 17.1 %fusion.14 = f32[64,9,1024,1]{2,0,1,3:T(8,128)S(1)} fusion(f32[8,17,64,1024]{3,2,1,0:T(8,128)} %bitcast.332, f32[9,8,64,64]{2,3,1,0:T(8,128)S(1)} %bitcast.351), kind=kOutput, calls=%fused_computation.14 | convolution fusion | flops 3623878656 | bytes 21495808 | tf_op jit(solution)/shard_map/knsc,ksr->nrc/dot_general | solution.py:64
  94.3 17.1 %fusion.2 = f32[64,9,1024,1]{2,0,1,3:T(8,128)S(1)} fusion(f32[8,17,64,1024]{3,2,1,0:T(8,128)} %bitcast.333, f32[9,8,64,64]{2,3,1,0:T(8,128)S(1)} %bitcast.352), kind=kOutput, calls=%fused_computation.2 | convolution fusion | flops 3623878656 | bytes 21495808 | tf_op jit(solution)/shard_map/knsc,ksr->nrc/dot_general | solution.py:64
  111.5 17.6 %fusion.4 = f32[64,9,1024,1]{2,0,1,3:T(8,128)S(1)} fusion(f32[8,17,64,1024]{3,2,1,0:T(8,128)} %bitcast.334, f32[9,8,64,64]{2,3,1,0:T(8,128)S(1)} %bitcast.353), kind=kOutput, calls=%fused_computation.4 | convolution fusion | flops 3623878656 | bytes 21495808 | tf_op jit(solution)/shard_map/knsc,ksr->nrc/dot_general | solution.py:64
  129.0 17.1 %fusion.6 = f32[64,9,1024,1]{2,0,1,3:T(8,128)S(1)} fusion(f32[8,17,64,1024]{3,2,1,0:T(8,128)} %bitcast.335, f32[9,8,64,64]{2,3,1,0:T(8,128)S(1)} %bitcast.354), kind=kOutput, calls=%fused_computation.6 | convolution fusion | flops 3623878656 | bytes 21495808 | tf_op jit(solution)/shard_map/knsc,ksr->nrc/dot_general | solution.py:64
  146.2 17.9 %fusion.8 = f32[64,9,1024,1]{2,0,1,3:T(8,128)} fusion(f32[8,17,64,1024]{3,2,1,0:T(8,128)} %bitcast.336, f32[9,8,64,64]{2,3,1,0:T(8,128)S(1)} %bitcast.355), kind=kOutput, calls=%fused_computation.8 | convolution fusion | flops 3623878656 | bytes 21495808 | tf_op jit(solution)/shard_map/knsc,ksr->nrc/dot_general | solution.py:64
  164.1 19.3 %fusion.18 = f32[9,64,1024]{2,1,0:T(8,128)S(1)} fusion(f32[64,9,1024,1]{2,0,1,3:T(8,128)S(1)} %fusion, f32[64,9,1024,1]{2,0,1,3:T(8,128)S(1)} %fusion.2, f32[64,9,1024,1]{2,0,1,3:T(8,128)S(1)} %fusion.4, f32[64,9,1024,1]{2,0,1,3:T(8,128)S(1)} %fusion.6, f32[64,9,1024,1]{2,0,1,3:T(8,128)} %fusion.8, f32[64,9,1024,1]{2,0,1,3:T(8,128)S(1)} %fusion.10, ...), kind=kOutput, calls=%fused_computation.21 | convolution fusion | flops 3628597248 | bytes 40370176 | tf_op jit(solution)/shard_map/knsc,ksr->nrc/dot_general | solution.py:64
  186.7 3.4 collective-permute-start.2
  190.1 4.4 collective-permute-start.3
  194.5 3.5 collective-permute-start.4
  200.1 6.6 %reshape.113 = f32[8,128,767]{2,1,0:T(8,128)} reshape(f32[8,98176]{1,0:T(8,128)} %slice.274) | data formatting | bytes 6283264 | tf_op jit(solution)/shard_map/reshape | solution.py:31
  215.4 5.3 %select_maximum_fusion = f32[8,64,2560]{2,1,0:T(8,128)} fusion(f32[8,64,1024]{2,1,0:T(8,128)} %broadcast_multiply_fusion, f32[8,64,1024]{2,1,0:T(8,128)} %collective-permute-done), kind=kLoop, calls=%fused_computation.18 | loop fusion | flops 5242880 | bytes 9437184 | tf_op jit(solution)/shard_map/concatenate | solution.py:89
  220.7 7.2 %reshape.112 = f32[8,64,20,128]{3,2,1,0:T(8,128)} reshape(f32[8,64,2560]{2,1,0:T(8,128)} %select_maximum_fusion) | data formatting | bytes 10485760 | tf_op jit(solution)/shard_map/reshape | solution.py:38
  227.9 4.2 fusion.39
  232.1 4.0 fusion.42
  236.2 3.5 fusion.45
  249.9 14.0 %collective-permute-done.7 = f32[64,1024]{1,0:T(8,128)S(1)} collective-permute-done((f32[64,1024]{1,0:T(8,128)S(1)}, f32[64,1024]{1,0:T(8,128)S(1)}, u32[]{:S(2)}, u32[]{:S(2)}) %collective-permute-start.7) | collective-permute-done | bytes 262176 | tf_op jit(solution)/shard_map/ppermute | solution.py:15
  264.0 4.4 collective-permute-done.8
  268.4 3.6 multiply_reduce_fusion.1
  274.4 52.1 %psum.14 = f32[]{:T(128)} all-reduce(f32[]{:T(128)S(6)} %add.173), channel_id=1, replica_groups=mesh['row'=16,'col'=2] {'row','col'}, use_global_device_ids=true, to_apply=%region_2.3 | all-reduce | flops 1 | bytes 8 | tf_op jit(solution)/shard_map/psum | solution.py:152
  340.9 4.2 fusion.102
  361.3 2.8 fusion.100
  365.4 2.8 fusion.94
  375.4 2.8 fusion.92
  381.9 3.3 collective-permute-done.17
  385.3 5.2 %multiply_reduce_fusion = (f32[]{:T(128)}, f32[8,64,1024]{2,1,0:T(8,128)}) fusion(f32[8,64,1024]{2,1,0:T(8,128)S(1)} %copy-done.5, f32[]{:T(128)S(6)} %sqrt.9, f32[64,1024]{1,0:T(8,128)S(1)} %collective-permute-done.17, f32[9,8,64,64]{2,3,1,0:T(8,128)S(1)} %bitcast.365, f32[8,64,1024]{2,1,0:T(8,128)S(1)} %fusion.88, f32[8,64,1024]{2,1,0:T(8,128)S(1)} %fusion.90, ...), kind=kOutput, calls=%fused_computation.44 | convolution fusion | flops 409993216 | bytes 23855112 | tf_op jit(solution)/shard_map/njc,krj->knrc/dot_general | solution.py:75
  390.5 56.8 %psum.15 = f32[]{:T(128)} all-reduce(f32[]{:T(128)} %get-tuple-element.36), channel_id=1, replica_groups=mesh['row'=16,'col'=2] {'row','col'}, use_global_device_ids=true, to_apply=%region_4.5 | all-reduce | flops 1 | bytes 8 | tf_op jit(solution)/shard_map/psum | solution.py:160
  448.1 6.5 %multiply_subtract_fusion = (f32[8,64,1024]{2,1,0:T(8,128)}, f32[8,64,1024]{2,1,0:T(8,128)}, f32[8,64,1024]{2,1,0:T(8,128)}) fusion(f32[8,64,1024]{2,1,0:T(8,128)} %param.12, f32[]{:T(128)S(6)} %div.40, f32[8,64,1024]{2,1,0:T(8,128)} %get-tuple-element.37, f32[]{:T(128)S(6)} %sqrt.11, f32[8,64,1024]{2,1,0:T(8,128)} %param.11, f32[]{:T(128)S(6)} %div.33), kind=kLoop, calls=%fused_computation.43 | loop fusion | flops 2621440 | bytes 12582924 | tf_op jit(solution)/shard_map/sub | solution.py:168
  (100 shorter events, 72.4 us)
Async XLA Ops:
  1.6 17.7 %copy-start.6 = (f32[64,1024]{1,0:T(8,128)}, f32[64,1024]{1,0:T(8,128)S(1)}, u32[]{:S(2)}) copy-start(f32[64,1024]{1,0:T(8,128)S(1)} %convert_element_type.21) | copy-start | bytes 786436
  4.9 14.4 %copy-start.17 = (f32[8,512]{1,0:T(8,128)S(1)}, f32[8,512]{1,0:T(8,128)}, u32[]{:S(2)}) copy-start(f32[8,512]{1,0:T(8,128)} %param.18) | copy-start | bytes 49156
  5.0 208.4 %collective-permute-start = (f32[8,64,1024]{2,1,0:T(8,128)}, f32[8,64,1024]{2,1,0:T(8,128)}, u32[]{:S(2)}, u32[]{:S(2)}) collective-permute-start(f32[8,64,1024]{2,1,0:T(8,128)} %broadcast_multiply_fusion), channel_id=1, source_target_pairs={{0,1},{2,3},{4,5},{6,7},{8,9},{10,11},{12,13},{14,15},{16,17},{18,... | collective-permute-start | bytes 6291464 | tf_op jit(solution)/shard_map/ppermute | solution.py:15
  24.6 139.4 %copy-start.1 = (f32[8,64,9,64]{1,3,0,2:T(8,128)}, f32[8,64,9,64]{1,3,0,2:T(8,128)S(1)}, u32[]{:S(2)}) copy-start(f32[8,64,9,64]{1,3,0,2:T(8,128)S(1)} %copy.159) | copy-start | bytes 3538948
  183.4 14.8 %copy-start.3 = (f32[9,64,1024]{2,1,0:T(8,128)}, f32[9,64,1024]{2,1,0:T(8,128)S(1)}, u32[]{:S(2)}) copy-start(f32[9,64,1024]{2,1,0:T(8,128)S(1)} %fusion.18) | copy-start | bytes 7077892
  183.4 14.6 %copy-start.18 = (f32[8,512]{1,0:T(8,128)S(1)}, f32[8,512]{1,0:T(8,128)}, u32[]{:S(2)}) copy-start(f32[8,512]{1,0:T(8,128)} %param.17) | copy-start | bytes 49156
  184.8 56.7 %collective-permute-start.1 = (f32[64,1024]{1,0:T(8,128)}, f32[64,1024]{1,0:T(8,128)S(1)}, u32[]{:S(2)}, u32[]{:S(2)}) collective-permute-start(f32[64,1024]{1,0:T(8,128)} %get-tuple-element.15), channel_id=1, source_target_pairs={{0,2},{2,4},{4,6},{6,8},{8,10},{10,12},{12,14},{14,16},{16,18},{18... | collective-permute-start | bytes 786440 | tf_op jit(solution)/shard_map/ppermute | solution.py:15
  186.7 56.6 %collective-permute-start.2 = (f32[64,1024]{1,0:T(8,128)}, f32[64,1024]{1,0:T(8,128)}, u32[]{:S(2)}, u32[]{:S(2)}) collective-permute-start(f32[64,1024]{1,0:T(8,128)} %get-tuple-element.22), channel_id=1, source_target_pairs={{0,4},{2,6},{4,8},{6,10},{8,12},{10,14},{12,16},{14,18},{16,20},{1... | collective-permute-start | bytes 786440 | tf_op jit(solution)/shard_map/ppermute | solution.py:15
  190.1 54.5 %collective-permute-start.3 = (f32[64,1024]{1,0:T(8,128)}, f32[64,1024]{1,0:T(8,128)}, u32[]{:S(2)}, u32[]{:S(2)}) collective-permute-start(f32[64,1024]{1,0:T(8,128)} %get-tuple-element.21), channel_id=1, source_target_pairs={{0,6},{2,8},{4,10},{6,12},{8,14},{10,16},{12,18},{14,20},{16,22},{... | collective-permute-start | bytes 786440 | tf_op jit(solution)/shard_map/ppermute | solution.py:15
  194.5 53.3 %collective-permute-start.4 = (f32[64,1024]{1,0:T(8,128)}, f32[64,1024]{1,0:T(8,128)}, u32[]{:S(2)}, u32[]{:S(2)}) collective-permute-start(f32[64,1024]{1,0:T(8,128)} %get-tuple-element.20), channel_id=1, source_target_pairs={{0,8},{2,10},{4,12},{6,14},{8,16},{10,18},{12,20},{14,22},{16,24},... | collective-permute-start | bytes 786440 | tf_op jit(solution)/shard_map/ppermute | solution.py:15
  213.4 34.4 %collective-permute-start.5 = (f32[64,1024]{1,0:T(8,128)}, f32[64,1024]{1,0:T(8,128)}, u32[]{:S(2)}, u32[]{:S(2)}) collective-permute-start(f32[64,1024]{1,0:T(8,128)} %get-tuple-element.19), channel_id=1, source_target_pairs={{0,10},{2,12},{4,14},{6,16},{8,18},{10,20},{12,22},{14,24},{16,26}... | collective-permute-start | bytes 786440 | tf_op jit(solution)/shard_map/ppermute | solution.py:15
  227.9 11.7 %copy-start = (f32[8,64,20,128]{3,2,1,0:T(8,128)S(1)}, f32[8,64,20,128]{3,2,1,0:T(8,128)}, u32[]{:S(2)}) copy-start(f32[8,64,20,128]{3,2,1,0:T(8,128)} %reshape.112) | copy-start | bytes 15728644
  236.1 7.1 %copy-start.15 = (f32[64,1024]{1,0:T(8,128)S(1)}, f32[64,1024]{1,0:T(8,128)}, u32[]{:S(2)}) copy-start(f32[64,1024]{1,0:T(8,128)} %get-tuple-element.17) | copy-start | bytes 786436
  236.1 8.5 %copy-start.14 = (f32[64,1024]{1,0:T(8,128)S(1)}, f32[64,1024]{1,0:T(8,128)}, u32[]{:S(2)}) copy-start(f32[64,1024]{1,0:T(8,128)} %get-tuple-element.16) | copy-start | bytes 786436
  241.4 26.9 %copy-start.8 = (s32[64,1024]{1,0:T(8,128)S(1)}, s32[64,1024]{1,0:T(8,128)}, u32[]{:S(2)}) copy-start(s32[64,1024]{1,0:T(8,128)} %param.20) | copy-start | bytes 786436
  241.5 26.9 %copy-start.9 = (s32[64,1024]{1,0:T(8,128)S(1)}, s32[64,1024]{1,0:T(8,128)}, u32[]{:S(2)}) copy-start(s32[64,1024]{1,0:T(8,128)} %param.21) | copy-start | bytes 786436
  241.5 26.9 %copy-start.11 = (f32[64,1024]{1,0:T(8,128)S(1)}, f32[64,1024]{1,0:T(8,128)}, u32[]{:S(2)}) copy-start(f32[64,1024]{1,0:T(8,128)} %param.15) | copy-start | bytes 786436
  241.5 26.9 %copy-start.12 = (f32[64,1024]{1,0:T(8,128)S(1)}, f32[64,1024]{1,0:T(8,128)}, u32[]{:S(2)}) copy-start(f32[64,1024]{1,0:T(8,128)} %param.14) | copy-start | bytes 786436
  241.5 26.9 %copy-start.13 = (f32[64,1024]{1,0:T(8,128)}, f32[64,1024]{1,0:T(8,128)S(1)}, u32[]{:S(2)}) copy-start(f32[64,1024]{1,0:T(8,128)S(1)} %collective-permute-done.1) | copy-start | bytes 786436
  241.5 8.4 %collective-permute-start.6 = (f32[64,1024]{1,0:T(8,128)S(1)}, f32[64,1024]{1,0:T(8,128)S(1)}, u32[]{:S(2)}, u32[]{:S(2)}) collective-permute-start(f32[64,1024]{1,0:T(8,128)S(1)} %copy-done.16), channel_id=1, source_target_pairs={{0,12},{2,14},{4,16},{6,18},{8,20},{10,22},{12,24},{14,26},{16,28}... | collective-permute-start | bytes 786440 | tf_op jit(solution)/shard_map/ppermute | solution.py:15
  243.3 20.7 %collective-permute-start.7 = (f32[64,1024]{1,0:T(8,128)S(1)}, f32[64,1024]{1,0:T(8,128)S(1)}, u32[]{:S(2)}, u32[]{:S(2)}) collective-permute-start(f32[64,1024]{1,0:T(8,128)S(1)} %copy-done.15), channel_id=1, source_target_pairs={{0,14},{2,16},{4,18},{6,20},{8,22},{10,24},{12,26},{14,28},{16,30}... | collective-permute-start | bytes 786440 | tf_op jit(solution)/shard_map/ppermute | solution.py:15
  244.6 23.8 %collective-permute-start.8 = (f32[64,1024]{1,0:T(8,128)S(1)}, f32[64,1024]{1,0:T(8,128)S(1)}, u32[]{:S(2)}, u32[]{:S(2)}) collective-permute-start(f32[64,1024]{1,0:T(8,128)S(1)} %copy-done.14), channel_id=1, source_target_pairs={{0,16},{2,18},{4,20},{6,22},{8,24},{10,26},{12,28},{14,30},{1,17},... | collective-permute-start | bytes 786440 | tf_op jit(solution)/shard_map/ppermute | solution.py:15
  329.2 19.0 %copy-start.10 = (f32[64,1024]{1,0:T(8,128)S(1)}, f32[64,1024]{1,0:T(8,128)}, u32[]{:S(2)}) copy-start(f32[64,1024]{1,0:T(8,128)} %get-tuple-element.29) | copy-start | bytes 786436
  329.2 30.8 %collective-permute-start.10 = (f32[64,1024]{1,0:T(8,128)}, f32[64,1024]{1,0:T(8,128)}, u32[]{:S(2)}, u32[]{:S(2)}) collective-permute-start(f32[64,1024]{1,0:T(8,128)} %get-tuple-element.7), channel_id=1, source_target_pairs={{2,0},{4,2},{6,4},{8,6},{10,8},{12,10},{14,12},{16,14},{18,16},{20... | collective-permute-start | bytes 786440 | tf_op jit(solution)/shard_map/ppermute | solution.py:15
  331.3 32.9 %collective-permute-start.13 = (f32[64,1024]{1,0:T(8,128)}, f32[64,1024]{1,0:T(8,128)}, u32[]{:S(2)}, u32[]{:S(2)}) collective-permute-start(f32[64,1024]{1,0:T(8,128)} %get-tuple-element.7), channel_id=1, source_target_pairs={{8,0},{10,2},{12,4},{14,6},{16,8},{18,10},{20,12},{22,14},{24,16},... | collective-permute-start | bytes 786440 | tf_op jit(solution)/shard_map/ppermute | solution.py:15
  333.2 35.1 %collective-permute-start.12 = (f32[64,1024]{1,0:T(8,128)}, f32[64,1024]{1,0:T(8,128)}, u32[]{:S(2)}, u32[]{:S(2)}) collective-permute-start(f32[64,1024]{1,0:T(8,128)} %get-tuple-element.7), channel_id=1, source_target_pairs={{6,0},{8,2},{10,4},{12,6},{14,8},{16,10},{18,12},{20,14},{22,16},{... | collective-permute-start | bytes 786440 | tf_op jit(solution)/shard_map/ppermute | solution.py:15
  335.1 37.5 %collective-permute-start.11 = (f32[64,1024]{1,0:T(8,128)}, f32[64,1024]{1,0:T(8,128)}, u32[]{:S(2)}, u32[]{:S(2)}) collective-permute-start(f32[64,1024]{1,0:T(8,128)} %get-tuple-element.7), channel_id=1, source_target_pairs={{4,0},{6,2},{8,4},{10,6},{12,8},{14,10},{16,12},{18,14},{20,16},{2... | collective-permute-start | bytes 786440 | tf_op jit(solution)/shard_map/ppermute | solution.py:15
  338.4 8.6 %collective-permute-start.9 = (f32[64,1024]{1,0:T(8,128)}, f32[64,1024]{1,0:T(8,128)S(1)}, u32[]{:S(2)}, u32[]{:S(2)}) collective-permute-start(f32[64,1024]{1,0:T(8,128)} %get-tuple-element.29), channel_id=1, source_target_pairs={{1,0},{3,2},{5,4},{7,6},{9,8},{11,10},{13,12},{15,14},{17,16},{19,... | collective-permute-start | bytes 786440 | tf_op jit(solution)/shard_map/ppermute | solution.py:15
  347.0 28.4 %collective-permute-start.14 = (f32[64,1024]{1,0:T(8,128)}, f32[64,1024]{1,0:T(8,128)}, u32[]{:S(2)}, u32[]{:S(2)}) collective-permute-start(f32[64,1024]{1,0:T(8,128)} %get-tuple-element.7), channel_id=1, source_target_pairs={{10,0},{12,2},{14,4},{16,6},{18,8},{20,10},{22,12},{24,14},{26,16}... | collective-permute-start | bytes 786440 | tf_op jit(solution)/shard_map/ppermute | solution.py:15
  360.0 18.2 %collective-permute-start.15 = (f32[64,1024]{1,0:T(8,128)}, f32[64,1024]{1,0:T(8,128)S(1)}, u32[]{:S(2)}, u32[]{:S(2)}) collective-permute-start(f32[64,1024]{1,0:T(8,128)} %get-tuple-element.7), channel_id=1, source_target_pairs={{12,0},{14,2},{16,4},{18,6},{20,8},{22,10},{24,12},{26,14},{28,16}... | collective-permute-start | bytes 786440 | tf_op jit(solution)/shard_map/ppermute | solution.py:15
  364.1 15.9 %collective-permute-start.16 = (f32[64,1024]{1,0:T(8,128)}, f32[64,1024]{1,0:T(8,128)S(1)}, u32[]{:S(2)}, u32[]{:S(2)}) collective-permute-start(f32[64,1024]{1,0:T(8,128)} %get-tuple-element.7), channel_id=1, source_target_pairs={{14,0},{16,2},{18,4},{20,6},{22,8},{24,10},{26,12},{28,14},{30,16}... | collective-permute-start | bytes 786440 | tf_op jit(solution)/shard_map/ppermute | solution.py:15
  368.3 17.0 %collective-permute-start.17 = (f32[64,1024]{1,0:T(8,128)}, f32[64,1024]{1,0:T(8,128)S(1)}, u32[]{:S(2)}, u32[]{:S(2)}) collective-permute-start(f32[64,1024]{1,0:T(8,128)} %get-tuple-element.7), channel_id=1, source_target_pairs={{16,0},{18,2},{20,4},{22,6},{24,8},{26,10},{28,12},{30,14},{17,1},... | collective-permute-start | bytes 786440 | tf_op jit(solution)/shard_map/ppermute | solution.py:15
  (7 other events, 34.1 us)
where the time goes:
time: 464 us; the launch traced here: 455 us
  matrix products  211 us (45%)
  blocking collectives  109 us (23%)
  local copies, waits for them, and re-layouts  43.5 us (9%)
  starting transfers between devices  36.6 us (8%)
  waiting for transfers between devices  25.8 us (6%)
  other arithmetic  22.5 us (5%)
  between operations  6.89 us (1%)
    dot_general x9, matrix products, rows_forward(): jnp.einsum('knsc,ksr->nrc', picked, table[lead], precision=precise)  159 us
    psum x1, blocking collectives, body(): lax.psum(jnp.sum(raw_v * raw_v), ('row', 'col')) + epsilon  56.8 us
    psum x1, blocking collectives, body(): lax.psum(jnp.sum(raw_a * raw_a) + jnp.sum(raw_b * raw_b), ('row', 'col'))  52.1 us
    ppermute x18, starting transfers between devices, shifted(): return lax.ppermute(block, axis, route)  36.6 us
    dot_general x9, matrix products, rows_adjoint(): jnp.einsum('njc,krj->knrc', picked, table[lead], precision=precise)  27.1 us
    ppermute x18, waiting for transfers between devices, shifted(): return lax.ppermute(block, axis, route)  25.8 us
    dot_general x5, matrix products, cols_forward(): jnp.einsum('krns,ksc->rnc', picked, table[lead], precision=precise)  15.3 us
    pad x1, local copies, waits for them, and re-layouts, forward(): jnp.pad(source, ((0, 0), (row_lead * row_width, row_depth * rows_here), (...  13 us
  transfers between devices with their start and end apart: 18, of which 5 were waited for; matrix products, arithmetic and copies ran while one was open for 56% of the time, Pallas kernels for 0%

commit v1 on v0

v1 whole, which is shorter than its diff:
```python
import functools
import math

import jax
import jax.numpy as jnp
from jax import lax
from jax.experimental import pallas as pl
from jax.experimental.pallas import tpu as pltpu
from jax.sharding import PartitionSpec as P

epsilon = 1e-12
LANES = 128
VMEM_BYTES = 40 * 1024 * 1024


def split(values):
    high = values.astype(jnp.bfloat16)
    return high, (values - high.astype(jnp.float32)).astype(jnp.bfloat16)


def dot3(left, right, dims):
    def dot(a, b):
        return lax.dot_general(a, b, (dims, ((), ())), preferred_element_type=jnp.float32)

    return dot(left[0], right[0]) + (dot(left[0], right[1]) + dot(left[1], right[0]))


def band_tiles(profile_ref, k, rows):
    length = profile_ref.shape[1]
    count = length // LANES
    row = lax.broadcasted_iota(jnp.int32, (rows, LANES), 0)
    lane = lax.broadcasted_iota(jnp.int32, (rows, LANES), 1)
    zero = jnp.zeros((rows, LANES), jnp.float32)
    rolled = []
    for e in range(count):
        piece = profile_ref[k : k + 1, e * LANES : (e + 1) * LANES]
        wide = jnp.broadcast_to(piece, (rows, LANES))
        rolled.append(pltpu.roll(wide, 0, 1, stride=1, stride_axis=0))
    inside = lane >= row
    for e in range(count + 1):
        ahead = rolled[e] if e < count else zero
        behind = rolled[e - 1] if e > 0 else zero
        yield e, jnp.where(inside, ahead, behind)


def rows_forward_kernel(depth, place_ref, basis_ref, mask_ref, profile_ref, keep_ref, send_ref, high_ref, low_ref):
    maps, rows, width = basis_ref.shape

    @pl.when(pl.program_id(0) == 0)
    def _():
        group = max(1, LANES // rows)
        for first in range(0, maps, group):
            members = [list(band_tiles(profile_ref, k, rows)) for k in range(first, first + group)]
            for e in range(len(members[0])):
                tile = jnp.concatenate([member[e][1] for member in members], axis=0)
                high, low = split(tile.T)
                place = (slice(e * LANES, (e + 1) * LANES), slice(first * rows, (first + group) * rows))
                high_ref[place] = high
                low_ref[place] = low

    masked = mask_ref[...].astype(jnp.float32)
    source = (basis_ref[...] * masked[None]).reshape(maps * rows, width)
    used = (depth + 1) * rows
    table = (high_ref[:used], low_ref[:used])
    total = dot3(table, split(source), ((1,), (0,)))
    core = place_ref[0]
    pairs = send_ref.shape[0]
    send_ref[pl.ds((pairs - 1) * (1 - core), 1)] = jnp.zeros((1, rows, width), jnp.float32)
    for d in range(depth + 1):
        block = total[d * rows : (d + 1) * rows]
        if d % 2 == 0:
            keep_ref[d // 2] = block
        else:
            send_ref[pl.ds(d // 2 + core, 1)] = block[None]


def rows_forward(basis, mask, profile, place, depth):
    maps, rows, columns = basis.shape
    width = math.gcd(256, columns)
    table_rows = (profile.shape[1] // LANES + 1) * LANES
    pairs = (depth + 1) // 2 + 1
    block = pl.BlockSpec((pairs, rows, width), lambda i, place: (0, 0, i))
    return pl.pallas_call(
        functools.partial(rows_forward_kernel, depth),
        grid_spec=pltpu.PrefetchScalarGridSpec(
            num_scalar_prefetch=1,
            grid=(columns // width,),
            in_specs=[
                pl.BlockSpec((maps, rows, width), lambda i, place: (0, 0, i)),
                pl.BlockSpec((rows, width), lambda i, place: (0, i)),
                pl.BlockSpec(profile.shape, lambda i, place: (0, 0)),
            ],
            out_specs=[block, block],
            scratch_shapes=[pltpu.VMEM((table_rows, maps * rows), jnp.bfloat16)] * 2,
        ),
        out_shape=[jax.ShapeDtypeStruct((pairs, rows, columns), jnp.float32)] * 2,
        compiler_params=pltpu.CompilerParams(vmem_limit_bytes=VMEM_BYTES),
        cost_estimate=pl.CostEstimate(
            flops=6 * (depth + 1) * rows * maps * rows * columns,
            bytes_accessed=4 * (maps + 1 + 2 * pairs) * rows * columns,
            transcendentals=0,
        ),
        name="rows_forward",
    )(place, basis, mask, profile)


def cols_forward_kernel(basis_ref, mask_ref, profile_ref, own_ref, halo_ref, high_ref, low_ref, left_high, left_low, total):
    maps, rows, columns = basis_ref.shape
    for k in range(maps):
        for e, tile in band_tiles(profile_ref, k, LANES):
            high, low = split(tile)
            place = (slice(k * LANES, (k + 1) * LANES), slice(e * LANES, (e + 1) * LANES))
            high_ref[place] = high
            low_ref[place] = low
    blocks = columns // LANES
    for n in range(blocks):
        lanes = slice(n * LANES, (n + 1) * LANES)
        masked = mask_ref[:, lanes].astype(jnp.float32)
        for k in range(maps):
            high, low = split(basis_ref[k, :, lanes] * masked)
            place = (slice(n * rows, (n + 1) * rows), slice(k * LANES, (k + 1) * LANES))
            left_high[place] = high
            left_low[place] = low
    reach = high_ref.shape[1]
    total[...] = jnp.zeros_like(total)
    spread = dot3((left_high[...], left_low[...]), (high_ref[...], low_ref[...]), ((1,), (0,)))
    for n in range(blocks):
        total[:, n * LANES : n * LANES + reach] += spread[n * rows : (n + 1) * rows]
    own_ref[...] = total[:, :columns]
    halo_ref[...] = total[:, columns:]


def cols_forward(basis, mask, profile):
    maps, rows, columns = basis.shape
    length = profile.shape[1]
    reach = length + LANES
    table = jax.ShapeDtypeStruct((maps * LANES, reach), jnp.bfloat16)
    stack = pltpu.VMEM((columns // LANES * rows, maps * LANES), jnp.bfloat16)
    return pl.pallas_call(
        cols_forward_kernel,
        out_shape=[
            jax.ShapeDtypeStruct((rows, columns), jnp.float32),
            jax.ShapeDtypeStruct((rows, length), jnp.float32),
            table,
            table,
        ],
        scratch_shapes=[stack, stack, pltpu.VMEM((rows, columns + length), jnp.float32)],
        compiler_params=pltpu.CompilerParams(vmem_limit_bytes=VMEM_BYTES),
        cost_estimate=pl.CostEstimate(
            flops=6 * rows * columns * maps * reach,
            bytes_accessed=4 * (maps + 3) * rows * columns,
            transcendentals=0,
        ),
        name="cols_forward",
    )(basis, mask, profile)


def cols_adjoint_kernel(image_ref, halo_ref, high_ref, low_ref, grad_ref, left_high, left_low):
    maps, rows, columns = grad_ref.shape
    reach = high_ref.shape[1]
    blocks = columns // LANES
    pieces = reach // LANES
    for b in range(blocks + pieces - 1):
        if b < blocks:
            tile = image_ref[:, b * LANES : (b + 1) * LANES]
        else:
            tile = halo_ref[:, (b - blocks) * LANES : (b - blocks + 1) * LANES]
        high, low = split(tile)
        for m in range(max(0, b - pieces + 1), min(blocks, b + 1)):
            place = (slice(m * rows, (m + 1) * rows), slice((b - m) * LANES, (b - m + 1) * LANES))
            left_high[place] = high
            left_low[place] = low
    for k in range(maps):
        band = slice(k * LANES, (k + 1) * LANES)
        spread = dot3((left_high[...], left_low[...]), (high_ref[band], low_ref[band]), ((1,), (1,)))
        for m in range(blocks):
            grad_ref[k, :, m * LANES : (m + 1) * LANES] = spread[m * rows : (m + 1) * rows]


def cols_adjoint(image, halo, high, low, maps):
    rows, columns = image.shape
    reach = high.shape[1]
    stack = pltpu.VMEM((columns // LANES * rows, reach), jnp.bfloat16)
    return pl.pallas_call(
        cols_adjoint_kernel,
        out_shape=jax.ShapeDtypeStruct((maps, rows, columns), jnp.float32),
        scratch_shapes=[stack, stack],
        compiler_params=pltpu.CompilerParams(vmem_limit_bytes=VMEM_BYTES),
        cost_estimate=pl.CostEstimate(
            flops=6 * rows * columns * maps * reach,
            bytes_accessed=4 * (maps + 3) * rows * columns,
            transcendentals=0,
        ),
        name="cols_adjoint",
    )(image, halo, high, low)


def rows_adjoint_kernel(evens, scale_ref, profile_ref, *refs):
    even_refs = refs[:evens]
    odd_ref, grad_ref, mask_ref, basis_ref, raw_ref, norm_ref, high_ref, low_ref, right_high, right_low = refs[evens:]
    maps, rows, width = grad_ref.shape
    depth = evens - 1 + odd_ref.shape[0]

    @pl.when(pl.program_id(0) == 0)
    def _():
        norm_ref[0, 0] = 0.0
        for k in range(maps):
            for e, tile in band_tiles(profile_ref, k, rows):
                high, low = split(tile)
                place = (slice(k * rows, (k + 1) * rows), slice(e * LANES, (e + 1) * LANES))
                high_ref[place] = high
                low_ref[place] = low
        filled = (depth + 1) * rows
        if right_high.shape[0] > filled:
            right_high[filled:] = jnp.zeros((right_high.shape[0] - filled, width), jnp.bfloat16)
            right_low[filled:] = jnp.zeros((right_high.shape[0] - filled, width), jnp.bfloat16)

    for d in range(depth + 1):
        high, low = split(even_refs[d // 2][...] if d % 2 == 0 else odd_ref[d // 2])
        right_high[d * rows : (d + 1) * rows] = high
        right_low[d * rows : (d + 1) * rows] = low
    table = (high_ref[...], low_ref[...])
    spread = dot3(table, (right_high[...], right_low[...]), ((1,), (0,)))
    beta = scale_ref[0]
    inverse = scale_ref[1]
    masked = mask_ref[...].astype(jnp.float32) * inverse
    raw = (spread.reshape(maps, rows, width) + grad_ref[...]) * masked[None] - beta * basis_ref[...]
    raw_ref[...] = raw
    norm_ref[0, 0] += jnp.sum(raw * raw)


def rows_adjoint(scale, profile, even, odd, grad, mask, basis):
    maps, rows, columns = basis.shape
    width = math.gcd(256, columns)
    reach = profile.shape[1] + LANES
    image = pl.BlockSpec((rows, width), lambda i, scale: (0, i))
    whole = pl.BlockSpec((maps, rows, width), lambda i, scale: (0, 0, i))
    return pl.pallas_call(
        functools.partial(rows_adjoint_kernel, len(even)),
        grid_spec=pltpu.PrefetchScalarGridSpec(
            num_scalar_prefetch=1,
            grid=(columns // width,),
            in_specs=[pl.BlockSpec(profile.shape, lambda i, scale: (0, 0))]
            + [image] * len(even)
            + [pl.BlockSpec((odd.shape[0], rows, width), lambda i, scale: (0, 0, i)), whole, image, whole],
            out_specs=[whole, pl.BlockSpec((1, 1), lambda i, scale: (0, 0), memory_space=pltpu.SMEM)],
            scratch_shapes=[pltpu.VMEM((maps * rows, reach), jnp.bfloat16)] * 2
            + [pltpu.VMEM((reach, width), jnp.bfloat16)] * 2,
        ),
        out_shape=[
            jax.ShapeDtypeStruct((maps, rows, columns), jnp.float32),
            jax.ShapeDtypeStruct((1, 1), jnp.float32),
        ],
        compiler_params=pltpu.CompilerParams(vmem_limit_bytes=VMEM_BYTES),
        cost_estimate=pl.CostEstimate(
            flops=6 * rows * columns * maps * reach,
            bytes_accessed=4 * (3 * maps + 12) * rows * columns,
            transcendentals=0,
        ),
        name="rows_adjoint",
    )(scale, profile, *even, odd, grad, mask, basis)


def shifted(block, axis, distance):
    devices = range(lax.axis_size(axis))
    return lax.ppermute(block, axis, [(i - distance, i) for i in devices if i - distance in devices])


def exchanged(block, axis, bit):
    return lax.ppermute(block, axis, [(i, i ^ bit) for i in range(lax.axis_size(axis))])


def total_over(value, axes):
    held = jnp.full((1, LANES), value, jnp.float32)
    for axis in axes:
        size = lax.axis_size(axis)
        bit = 1
        while bit < size:
            held = held + exchanged(held, axis, bit)
            bit *= 2
    return held[0, 0]


def total_at_once(value, axes):
    count = math.prod(lax.axis_size(axis) for axis in axes)
    copies = jnp.full((count, LANES), value, jnp.float32)
    return jnp.sum(lax.all_to_all(copies, axes, 0, 0, tiled=True)[:, 0])


def body(
    solution,
    search,
    basis,
    resid_a,
    resid_b,
    scalars,
    profile_a,
    profile_b,
    source_mask,
    weight_code,
    roll_code,
):
    alpha = scalars[0]
    phibar = scalars[1]
    rhobar = scalars[2]
    length = profile_a.shape[1]
    maps, rows_here, cols_here = basis.shape
    row_depth = -(-(length - 1) // rows_here)
    col_depth = -(-(length - 1) // cols_here)
    place = lax.axis_index("row")
    core = place % 2
    lower = (place // 2) % 2 == 0
    base = 1.0 / (1.0 + 0.25 * weight_code.astype(jnp.float32))
    weight_a = base * (roll_code != 2).astype(jnp.float32)
    weight_b = base * (roll_code != 1).astype(jnp.float32)

    keep, send = rows_forward(basis, source_mask, profile_b, core.reshape(1), row_depth)
    got = exchanged(send, "row", 1)
    pairs = [keep[m] + got[m] for m in range(keep.shape[0])]
    pair_depth = len(pairs) - 1
    four_depth = (pair_depth + 1) // 2
    zero = jnp.zeros((rows_here, cols_here), jnp.float32)
    odd_in = [zero] * (four_depth + 2)
    for m in reversed(range(1, pair_depth + 1, 2)):
        odd_in[m // 2 + 1] = exchanged(pairs[m], "row", 2)
    carried = zero
    for n in reversed(range(four_depth + 1)):
        mine = pairs[2 * n] if 2 * n <= pair_depth else zero
        level = mine + jnp.where(lower, odd_in[n], odd_in[n + 1])
        if n < four_depth:
            level = level + carried
        if n > 0:
            carried = shifted(level, "row", 4)
    image_b = level

    own, halo, table_high, table_low = cols_forward(basis, source_mask, profile_a)
    image_a = own
    for n in range(1, col_depth + 1):
        piece = halo[:, (n - 1) * cols_here : n * cols_here]
        piece = shifted(piece, "col", n)
        image_a = image_a + jnp.pad(piece, ((0, 0), (0, cols_here - piece.shape[1])))

    raw_a = weight_a * image_a - alpha * resid_a
    raw_b = weight_b * image_b - alpha * resid_b
    weighted_a = weight_a * raw_a
    weighted_b = weight_b * raw_b

    pieces = []
    for n in range(1, col_depth + 1):
        width = min(cols_here, length - (n - 1) * cols_here)
        pieces.append(shifted(weighted_a[:, :width], "col", -n))
    grad_a = cols_adjoint(weighted_a, jnp.concatenate(pieces, axis=1), table_high, table_low, maps)

    fours = [weighted_b]
    for n in range(four_depth):
        fours.append(shifted(fours[-1], "row", -4))
    evens = []
    for m in range(pair_depth + 1):
        if m % 2 == 0:
            evens.append(fours[m // 2])
        else:
            evens.append(exchanged(jnp.where(lower, fours[m // 2 + 1], fours[m // 2]), "row", 2))
    first = core == 0
    odd = jnp.stack([jnp.where(first, evens[m + 1], evens[m]) for m in range(pair_depth)])
    odd = exchanged(odd, "row", 1)

    square = total_over(jnp.sum(raw_a * raw_a) + jnp.sum(raw_b * raw_b), ("row", "col"))
    beta = jnp.sqrt(square + epsilon)
    scale = jnp.stack([beta, 1.0 / beta])
    raw_v, norm = rows_adjoint(scale, profile_b, evens, odd, grad_a, source_mask, basis)
    alpha_next = jnp.sqrt(total_at_once(norm[0, 0], ("row", "col")) + epsilon)

    next_resid_a = raw_a / beta
    next_resid_b = raw_b / beta
    next_basis = raw_v / alpha_next
    rho_total = jnp.sqrt(rhobar * rhobar + beta * beta)
    cosine = rhobar / rho_total
    sine = beta / rho_total
    theta = sine * alpha_next
    phi_value = cosine * phibar
    next_solution = solution + phi_value / rho_total * search
    next_search = next_basis - theta / rho_total * search
    return (next_solution, next_search, next_basis, next_resid_a, next_resid_b)


def solution(mesh):
    placed = (
        P(None, "row", "col"),
        P(None, "row", "col"),
        P(None, "row", "col"),
        P("row", "col"),
        P("row", "col"),
        P(),
        P(),
        P(),
        P("row", "col"),
        P("row", "col"),
        P("row", "col"),
    )
    return jax.shard_map(
        body,
        mesh=mesh,
        in_specs=placed,
        out_specs=(
            P(None, "row", "col"),
            P(None, "row", "col"),
            P(None, "row", "col"),
            P("row", "col"),
            P("row", "col"),
        ),
        check_vma=False,
    )
```

time: 464 us -> 135 us (0.29)
  the two profiles are of different devices: /device:TPU:12 before, /device:TPU:0 now
where the time goes in v1:
time: 135 us
  waiting for transfers between devices  52.8 us (39%)
  starting transfers between devices  34.1 us (25%)
  Pallas kernels  17.1 us (13%)
  other arithmetic  13.3 us (10%)
  local copies, waits for them, and re-layouts  11.6 us (9%)
  between operations  5.7 us (4%)
    ppermute x11, waiting for transfers between devices, exchanged(): lax.ppermute(block, axis, [(i, i ^ bit) for i in range(lax.axis_size(axis...  24.9 us
    ppermute x6, waiting for transfers between devices, shifted(): lax.ppermute(block, axis, [(i - distance, i) for i in devices if i - dist...  23.8 us
    ppermute x6, starting transfers between devices, shifted(): lax.ppermute(block, axis, [(i - distance, i) for i in devices if i - dist...  15.7 us
    ppermute x11, starting transfers between devices, exchanged(): lax.ppermute(block, axis, [(i, i ^ bit) for i in range(lax.axis_size(axis...  14.5 us
    unnamed x44, local copies, waits for them, and re-layouts  9.72 us
    pallas_call x1, Pallas kernels, rows_adjoint(): pl.pallas_call(functools.partial(rows_adjoint_kernel, len(even)), grid_sp...  5.72 us
    sub x1, other arithmetic, body(): next_search = next_basis - theta / rho_total * search  5.61 us
    pallas_call x1, Pallas kernels, cols_adjoint(): pl.pallas_call(cols_adjoint_kernel, out_shape=jax.ShapeDtypeStruct((maps,...  4.29 us
  transfers between devices with their start and end apart: 18, of which 15 were waited for; matrix products, arithmetic and copies ran while one was open for 3% of the time, Pallas kernels for 6%

profile of v1, /device:TPU:0, one launch (start us, length us, event | category | flops | bytes accessed | tf_op | source)
XLA Modules:
  0.0 134.7 jit_solution(8484639572482307424)
XLA Ops:
  0.7 1.6 %copy-done = f32[8,64,1024]{2,1,0:T(8,128)S(1)} copy-done((f32[8,64,1024]{2,1,0:T(8,128)S(1)}, f32[8,64,1024]{2,1,0:T(8,128)}, u32[]{:S(2)}) %copy-start) | copy-done | bytes 2097176
  3.9 3.7 %rows_forward.1 = (f32[5,64,1024]{2,1,0:T(8,128)S(1)}, f32[5,64,1024]{2,1,0:T(8,128)S(1)}) custom-call(s32[1]{0:T(128)} %bitcast.2.place_ref, f32[8,64,1024]{2,1,0:T(8,128)S(1)} %copy-done, s32[64,1024]{1,0:T(8,128)S(1)} %copy-done.5, f32[8,512]{1,0:T(8,128)S(1)} %copy-done.9), custom_call_target="tpu_custom_call" | custom-call | flops 1811939328 | bytes 4980736 | tf_op jit(solution)/shard_map/rows_forward/pallas_call | solution.py:83
  8.1 2.7 %collective-permute-done.1 = f32[5,64,1024]{2,1,0:T(8,128)S(1)} collective-permute-done((f32[5,64,1024]{2,1,0:T(8,128)S(1)}, f32[5,64,1024]{2,1,0:T(8,128)S(1)}, u32[]{:S(2)}, u32[]{:S(2)}) %collective-permute-start.1) | collective-permute-done | bytes 1310752 | tf_op jit(solution)/shard_map/ppermute | solution.py:270
  11.6 2.8 %collective-permute-start.3 = (f32[64,1024]{1,0:T(8,128)}, f32[64,1024]{1,0:T(8,128)S(1)}, u32[]{:S(2)}, u32[]{:S(2)}) collective-permute-start(f32[64,1024]{1,0:T(8,128)} %get-tuple-element.28), channel_id=1, source_target_pairs={{0,4},{2,6},{4,0},{6,2},{8,12},{10,14},{12,8},{14,10},{16,20},{18,... | collective-permute-start | bytes 786440 | tf_op jit(solution)/shard_map/ppermute | solution.py:270
  14.4 7.3 %collective-permute-done.3 = f32[64,1024]{1,0:T(8,128)S(1)} collective-permute-done((f32[64,1024]{1,0:T(8,128)}, f32[64,1024]{1,0:T(8,128)S(1)}, u32[]{:S(2)}, u32[]{:S(2)}) %collective-permute-start.3) | collective-permute-done | bytes 262176 | tf_op jit(solution)/shard_map/ppermute | solution.py:270
  21.8 4.0 %collective-permute-start.4 = (f32[64,1024]{1,0:T(8,128)S(1)}, f32[64,1024]{1,0:T(8,128)S(1)}, u32[]{:S(2)}, u32[]{:S(2)}) collective-permute-start(f32[64,1024]{1,0:T(8,128)S(1)} %fusion.1), channel_id=1, source_target_pairs={{0,8},{2,10},{4,12},{6,14},{8,16},{10,18},{12,20},{14,22},{16,24},... | collective-permute-start | bytes 786440 | tf_op jit(solution)/shard_map/ppermute | solution.py:266
  26.9 3.2 %collective-permute-done.4 = f32[64,1024]{1,0:T(8,128)S(1)} collective-permute-done((f32[64,1024]{1,0:T(8,128)S(1)}, f32[64,1024]{1,0:T(8,128)S(1)}, u32[]{:S(2)}, u32[]{:S(2)}) %collective-permute-start.4) | collective-permute-done | bytes 262176 | tf_op jit(solution)/shard_map/ppermute | solution.py:266
  30.1 4.4 %collective-permute-start.5 = (f32[64,1024]{1,0:T(8,128)S(1)}, f32[64,1024]{1,0:T(8,128)S(1)}, u32[]{:S(2)}, u32[]{:S(2)}) collective-permute-start(f32[64,1024]{1,0:T(8,128)S(1)} %fusion.5), channel_id=1, source_target_pairs={{0,8},{2,10},{4,12},{6,14},{8,16},{10,18},{12,20},{14,22},{16,24},... | collective-permute-start | bytes 786440 | tf_op jit(solution)/shard_map/ppermute | solution.py:266
  34.5 1.6 %copy-done.1 = f32[8,64,1024]{2,1,0:T(8,128)S(1)} copy-done((f32[8,64,1024]{2,1,0:T(8,128)S(1)}, f32[8,64,1024]{2,1,0:T(8,128)}, u32[]{:S(2)}) %copy-start.1) | copy-done | bytes 2097176
  36.1 3.4 %cols_forward.1 = (f32[64,1024]{1,0:T(8,128)S(1)}, f32[64,512]{1,0:T(8,128)S(1)}, bf16[1024,640]{1,0:T(8,128)(2,1)S(1)}, bf16[1024,640]{1,0:T(8,128)(2,1)S(1)}) custom-call(f32[8,64,1024]{2,1,0:T(8,128)S(1)} %copy-done.1, s32[64,1024]{1,0:T(8,128)S(1)} %copy-done.6, f32[8,512]{1,0:T(8,128)S(1)} %copy-done.8), custom_call_target="tpu_custom_call" | custom-call | flops 2013265920 | bytes 2883584 | tf_op jit(solution)/shard_map/cols_forward/pallas_call | solution.py:139
  39.6 3.4 %collective-permute-start = (f32[64,512]{1,0:T(8,128)S(1)}, f32[64,512]{1,0:T(8,128)S(1)}, u32[]{:S(2)}, u32[]{:S(2)}) collective-permute-start(f32[64,512]{1,0:T(8,128)S(1)} %get-tuple-element.14), channel_id=1, source_target_pairs={{0,1},{2,3},{4,5},{6,7},{8,9},{10,11},{12,13},{14,15},{16,17},{18,... | collective-permute-start | bytes 393224 | tf_op jit(solution)/shard_map/ppermute | solution.py:266
  43.7 1.9 %collective-permute-done = f32[64,512]{1,0:T(8,128)S(1)} collective-permute-done((f32[64,512]{1,0:T(8,128)S(1)}, f32[64,512]{1,0:T(8,128)S(1)}, u32[]{:S(2)}, u32[]{:S(2)}) %collective-permute-start) | collective-permute-done | bytes 131104 | tf_op jit(solution)/shard_map/ppermute | solution.py:266
  45.5 1.9 %fusion.13 = (f32[64,1024]{1,0:T(8,128)S(1)}, f32[64,1024]{1,0:T(8,128)S(1)}, f32[64,1024]{1,0:T(8,128)S(1)}, f32[64,1024]{1,0:T(8,128)S(1)}) fusion(s32[64,1024]{1,0:T(8,128)S(1)} %copy-done.17, s32[64,1024]{1,0:T(8,128)S(1)} %copy-done.18, f32[64,1024]{1,0:T(8,128)S(1)} %copy-done.19, f32[]{:T(128)} %bitcast.1, f32[64,1024]{1,0:T(8,128)S(1)} %collective-permute-done.5, ...), kind=kLoop, calls=%fused_computation.36 | loop fusion | flops 1376256 | bytes 3538949 | tf_op jit(solution)/shard_map/mul | solution.py:346
  48.7 7.2 %collective-permute-done.11.refs_2_ = f32[64,1024]{1,0:T(8,128)S(1)} collective-permute-done((f32[64,1024]{1,0:T(8,128)S(1)}, f32[64,1024]{1,0:T(8,128)S(1)}, u32[]{:S(2)}, u32[]{:S(2)}) %collective-permute-start.11) | collective-permute-done | bytes 262176 | tf_op jit(solution)/shard_map/ppermute | solution.py:266
  57.2 7.0 %collective-permute-done.13.refs_4_ = f32[64,1024]{1,0:T(8,128)S(1)} collective-permute-done((f32[64,1024]{1,0:T(8,128)S(1)}, f32[64,1024]{1,0:T(8,128)S(1)}, u32[]{:S(2)}, u32[]{:S(2)}) %collective-permute-start.13) | collective-permute-done | bytes 262176 | tf_op jit(solution)/shard_map/ppermute | solution.py:266
  64.2 1.6 %collective-permute-start.14 = (f32[64,1024]{1,0:T(8,128)S(1)}, f32[64,1024]{1,0:T(8,128)S(1)}, u32[]{:S(2)}, u32[]{:S(2)}) collective-permute-start(f32[64,1024]{1,0:T(8,128)S(1)} %get-tuple-element.36), channel_id=1, source_target_pairs={{0,4},{2,6},{4,0},{6,2},{8,12},{10,14},{12,8},{14,10},{16,20},{18,... | collective-permute-start | bytes 786440 | tf_op jit(solution)/shard_map/ppermute | solution.py:270
  66.3 4.3 %collective-permute-done.14.refs_3_ = f32[64,1024]{1,0:T(8,128)S(1)} collective-permute-done((f32[64,1024]{1,0:T(8,128)S(1)}, f32[64,1024]{1,0:T(8,128)S(1)}, u32[]{:S(2)}, u32[]{:S(2)}) %collective-permute-start.14) | collective-permute-done | bytes 262176 | tf_op jit(solution)/shard_map/ppermute | solution.py:270
  70.7 2.8 %collective-permute-done.12.refs_1_ = f32[64,1024]{1,0:T(8,128)S(1)} collective-permute-done((f32[64,1024]{1,0:T(8,128)S(1)}, f32[64,1024]{1,0:T(8,128)S(1)}, u32[]{:S(2)}, u32[]{:S(2)}) %collective-permute-start.12) | collective-permute-done | bytes 262176 | tf_op jit(solution)/shard_map/ppermute | solution.py:270
  78.0 1.5 %collective-permute-start.7 = (f32[1,128]{1,0:T(1,128)S(1)}, f32[1,128]{1,0:T(1,128)S(1)}, u32[]{:S(2)}, u32[]{:S(2)}) collective-permute-start(f32[1,128]{1,0:T(1,128)S(1)} %broadcast_add_fusion), channel_id=1, source_target_pairs={{0,4},{2,6},{4,0},{6,2},{8,12},{10,14},{12,8},{14,10},{16,20},{18,... | collective-permute-start | bytes 1544 | tf_op jit(solution)/shard_map/ppermute | solution.py:270
  79.5 2.1 %collective-permute-done.7 = f32[1,128]{1,0:T(1,128)S(1)} collective-permute-done((f32[1,128]{1,0:T(1,128)S(1)}, f32[1,128]{1,0:T(1,128)S(1)}, u32[]{:S(2)}, u32[]{:S(2)}) %collective-permute-start.7) | collective-permute-done | bytes 544 | tf_op jit(solution)/shard_map/ppermute | solution.py:270
  81.6 1.6 %collective-permute-start.8 = (f32[1,128]{1,0:T(1,128)S(1)}, f32[1,128]{1,0:T(1,128)S(1)}, u32[]{:S(2)}, u32[]{:S(2)}) collective-permute-start(f32[1,128]{1,0:T(1,128)S(1)} %fusion.16), channel_id=1, source_target_pairs={{0,8},{2,10},{4,12},{6,14},{8,0},{10,2},{12,4},{14,6},{16,24},{18,... | collective-permute-start | bytes 1544 | tf_op jit(solution)/shard_map/ppermute | solution.py:270
  83.2 2.0 %collective-permute-done.8 = f32[1,128]{1,0:T(1,128)S(1)} collective-permute-done((f32[1,128]{1,0:T(1,128)S(1)}, f32[1,128]{1,0:T(1,128)S(1)}, u32[]{:S(2)}, u32[]{:S(2)}) %collective-permute-start.8) | collective-permute-done | bytes 544 | tf_op jit(solution)/shard_map/ppermute | solution.py:270
  85.2 2.6 %collective-permute-start.9 = (f32[1,128]{1,0:T(1,128)S(1)}, f32[1,128]{1,0:T(1,128)S(1)}, u32[]{:S(2)}, u32[]{:S(2)}) collective-permute-start(f32[1,128]{1,0:T(1,128)S(1)} %add.114), channel_id=1, source_target_pairs={{0,16},{2,18},{4,20},{6,22},{8,24},{10,26},{12,28},{14,30},{16,0},... | collective-permute-start | bytes 1544 | tf_op jit(solution)/shard_map/ppermute | solution.py:270
  87.7 1.9 %collective-permute-done.9 = f32[1,128]{1,0:T(1,128)S(1)} collective-permute-done((f32[1,128]{1,0:T(1,128)S(1)}, f32[1,128]{1,0:T(1,128)S(1)}, u32[]{:S(2)}, u32[]{:S(2)}) %collective-permute-start.9) | collective-permute-done | bytes 544 | tf_op jit(solution)/shard_map/ppermute | solution.py:270
  89.6 2.7 %collective-permute-start.10 = (f32[1,128]{1,0:T(1,128)S(1)}, f32[1,128]{1,0:T(1,128)S(1)}, u32[]{:S(2)}, u32[]{:S(2)}) collective-permute-start(f32[1,128]{1,0:T(1,128)S(1)} %add.115), channel_id=1, source_target_pairs={{0,1},{1,0},{2,3},{3,2},{4,5},{5,4},{6,7},{7,6},{8,9},{9,8},{10,11... | collective-permute-start | bytes 1544 | tf_op jit(solution)/shard_map/ppermute | solution.py:270
  95.9 4.6 %collective-permute-done.16.halo_ref = f32[64,512]{1,0:T(8,128)S(1)} collective-permute-done((f32[64,512]{1,0:T(8,128)S(1)}, f32[64,512]{1,0:T(8,128)S(1)}, u32[]{:S(2)}, u32[]{:S(2)}) %collective-permute-start.16) | collective-permute-done | bytes 131104 | tf_op jit(solution)/shard_map/ppermute | solution.py:266
  103.2 4.3 %cols_adjoint.1.refs_6_ = f32[8,64,1024]{2,1,0:T(8,128)S(1)} custom-call(f32[64,1024]{1,0:T(8,128)S(1)} %get-tuple-element.30.image_ref, f32[64,512]{1,0:T(8,128)S(1)} %collective-permute-done.16.halo_ref, bf16[1024,640]{1,0:T(8,128)(2,1)S(1)} %copy-done.12, bf16[1024,640]{1,0:T(8,128)(2,1)S(1)} %copy-done.14), custom_call_target="tpu_custom_call" | custom-call | flops 2013265920 | bytes 2883584 | tf_op jit(solution)/shard_map/cols_adjoint/pallas_call | solution.py:184
  109.7 5.7 %rows_adjoint.1 = (f32[8,64,1024]{2,1,0:T(8,128)S(1)}, f32[1,1]{1,0:T(1,128)}) custom-call(f32[2]{0:T(128)S(1)} %pad_maximum_fusion.1.scale_ref, f32[8,512]{1,0:T(8,128)S(1)} %copy-done.10, f32[64,1024]{1,0:T(8,128)S(1)} %get-tuple-element.25.refs_0_, f32[64,1024]{1,0:T(8,128)S(1)} %collective-permute-done.12.refs_1_, ...), custom_call_target="tpu_custom_call" | custom-call | flops 2013265920 | bytes 9437184 | tf_op jit(solution)/shard_map/rows_adjoint/pallas_call | solution.py:238
  116.7 3.9 %all-to-all-start = ((f32[32,1,128]{2,1,0:T(1,128)}), f32[32,1,128]{2,1,0:T(1,128)S(1)}, u32[]{:S(2)}, u32[]{:S(2)}) async-start(f32[32,1,128]{2,1,0:T(1,128)} %broadcast_in_dim.8), calls=%async_computation | async-start | bytes 32768 | tf_op jit(solution)/shard_map/all_to_all | solution.py:287
  120.6 1.7 %broadcast_divide_fusion.2 = f32[64,1024]{1,0:T(8,128)} fusion(f32[64,1024]{1,0:T(8,128)} %copy-done.15, f32[]{:T(128)} %bitcast.8), kind=kLoop, calls=%fused_computation.32 | loop fusion | flops 65536 | bytes 524292 | tf_op jit(solution)/shard_map/div | solution.py:373
  123.6 4.1 %all-to-all-done = f32[32,1,128]{2,1,0:T(1,128)S(1)} async-done(((f32[32,1,128]{2,1,0:T(1,128)}), f32[32,1,128]{2,1,0:T(1,128)S(1)}, u32[]{:S(2)}, u32[]{:S(2)}) %all-to-all-start) | async-done | bytes 16416 | tf_op jit(solution)/shard_map/all_to_all | solution.py:287
  129.1 5.6 %multiply_subtract_fusion = (f32[8,64,1024]{2,1,0:T(8,128)}, f32[8,64,1024]{2,1,0:T(8,128)}, f32[8,64,1024]{2,1,0:T(8,128)}) fusion(f32[8,64,1024]{2,1,0:T(8,128)} %param.12, f32[]{:T(128)S(6)} %div.52, f32[8,64,1024]{2,1,0:T(8,128)S(1)} %get-tuple-element.19, f32[]{:T(128)S(6)} %sqrt.15, f32[8,64,1024]{2,1,0:T(8,128)} %param.11, f32[]{:T(128)S(6)} %div.47), kind=kLoop, calls=%fused_computation | loop fusion | flops 2621440 | bytes 12582924 | tf_op jit(solution)/shard_map/sub | solution.py:382
  (74 shorter events, 20.0 us)
Async XLA Ops:
  7.6 3.2 %collective-permute-start.1 = (f32[5,64,1024]{2,1,0:T(8,128)S(1)}, f32[5,64,1024]{2,1,0:T(8,128)S(1)}, u32[]{:S(2)}, u32[]{:S(2)}) collective-permute-start(f32[5,64,1024]{2,1,0:T(8,128)S(1)} %get-tuple-element.16), channel_id=1, source_target_pairs={{0,2},{2,0},{4,6},{6,4},{8,10},{10,8},{12,14},{14,12},{16,18},{18,... | collective-permute-start | bytes 3932168 | tf_op jit(solution)/shard_map/ppermute | solution.py:270
  10.8 19.3 %copy-start.16 = (f32[5,64,1024]{2,1,0:T(8,128)}, f32[5,64,1024]{2,1,0:T(8,128)S(1)}, u32[]{:S(2)}) copy-start(f32[5,64,1024]{2,1,0:T(8,128)S(1)} %collective-permute-done.1) | copy-start | bytes 3932164
  10.8 23.7 %copy-start.6 = (s32[64,1024]{1,0:T(8,128)S(1)}, s32[64,1024]{1,0:T(8,128)}, u32[]{:S(2)}) copy-start(s32[64,1024]{1,0:T(8,128)} %refs_7_.1) | copy-start | bytes 786436
  10.8 23.7 %copy-start.8 = (f32[8,512]{1,0:T(8,128)S(1)}, f32[8,512]{1,0:T(8,128)}, u32[]{:S(2)}) copy-start(f32[8,512]{1,0:T(8,128)} %profile_ref.3) | copy-start | bytes 49156
  11.6 10.2 %collective-permute-start.3 = (f32[64,1024]{1,0:T(8,128)}, f32[64,1024]{1,0:T(8,128)S(1)}, u32[]{:S(2)}, u32[]{:S(2)}) collective-permute-start(f32[64,1024]{1,0:T(8,128)} %get-tuple-element.28), channel_id=1, source_target_pairs={{0,4},{2,6},{4,0},{6,2},{8,12},{10,14},{12,8},{14,10},{16,20},{18,... | collective-permute-start | bytes 786440 | tf_op jit(solution)/shard_map/ppermute | solution.py:270
  14.4 12.4 %collective-permute-start.2 = (f32[64,1024]{1,0:T(8,128)S(1)}, f32[64,1024]{1,0:T(8,128)S(1)}, u32[]{:S(2)}, u32[]{:S(2)}) collective-permute-start(f32[64,1024]{1,0:T(8,128)S(1)} %get-tuple-element.27), channel_id=1, source_target_pairs={{0,4},{2,6},{4,0},{6,2},{8,12},{10,14},{12,8},{14,10},{16,20},{18,... | collective-permute-start | bytes 786440 | tf_op jit(solution)/shard_map/ppermute | solution.py:270
  21.8 8.2 %collective-permute-start.4 = (f32[64,1024]{1,0:T(8,128)S(1)}, f32[64,1024]{1,0:T(8,128)S(1)}, u32[]{:S(2)}, u32[]{:S(2)}) collective-permute-start(f32[64,1024]{1,0:T(8,128)S(1)} %fusion.1), channel_id=1, source_target_pairs={{0,8},{2,10},{4,12},{6,14},{8,16},{10,18},{12,20},{14,22},{16,24},... | collective-permute-start | bytes 786440 | tf_op jit(solution)/shard_map/ppermute | solution.py:266
  30.1 15.4 %collective-permute-start.5 = (f32[64,1024]{1,0:T(8,128)S(1)}, f32[64,1024]{1,0:T(8,128)S(1)}, u32[]{:S(2)}, u32[]{:S(2)}) collective-permute-start(f32[64,1024]{1,0:T(8,128)S(1)} %fusion.5), channel_id=1, source_target_pairs={{0,8},{2,10},{4,12},{6,14},{8,16},{10,18},{12,20},{14,22},{16,24},... | collective-permute-start | bytes 786440 | tf_op jit(solution)/shard_map/ppermute | solution.py:266
  36.1 6.9 %copy-start.21 = (f32[3]{0:T(128)S(1)}, f32[3]{0:T(128)}, u32[]{:S(2)}) copy-start(f32[3]{0:T(128)} %param.16) | copy-start | bytes 40
  36.1 9.4 %copy-start.17 = (s32[64,1024]{1,0:T(8,128)S(1)}, s32[64,1024]{1,0:T(8,128)}, u32[]{:S(2)}) copy-start(s32[64,1024]{1,0:T(8,128)} %param.21) | copy-start | bytes 786436
  36.1 9.4 %copy-start.18 = (s32[64,1024]{1,0:T(8,128)S(1)}, s32[64,1024]{1,0:T(8,128)}, u32[]{:S(2)}) copy-start(s32[64,1024]{1,0:T(8,128)} %param.20) | copy-start | bytes 786436
  36.1 9.4 %copy-start.19 = (f32[64,1024]{1,0:T(8,128)S(1)}, f32[64,1024]{1,0:T(8,128)}, u32[]{:S(2)}) copy-start(f32[64,1024]{1,0:T(8,128)} %param.15) | copy-start | bytes 786436
  36.1 9.4 %copy-start.20 = (f32[64,1024]{1,0:T(8,128)S(1)}, f32[64,1024]{1,0:T(8,128)}, u32[]{:S(2)}) copy-start(f32[64,1024]{1,0:T(8,128)} %param.14) | copy-start | bytes 786436
  39.6 24.7 %copy-start.11 = (bf16[1024,640]{1,0:T(8,128)(2,1)}, bf16[1024,640]{1,0:T(8,128)(2,1)S(1)}, u32[]{:S(2)}) copy-start(bf16[1024,640]{1,0:T(8,128)(2,1)S(1)} %get-tuple-element.17.high_ref) | copy-start | bytes 3932164
  39.6 24.7 %copy-start.13 = (bf16[1024,640]{1,0:T(8,128)(2,1)}, bf16[1024,640]{1,0:T(8,128)(2,1)S(1)}, u32[]{:S(2)}) copy-start(bf16[1024,640]{1,0:T(8,128)(2,1)S(1)} %get-tuple-element.18.low_ref) | copy-start | bytes 3932164
  39.6 5.9 %collective-permute-start = (f32[64,512]{1,0:T(8,128)S(1)}, f32[64,512]{1,0:T(8,128)S(1)}, u32[]{:S(2)}, u32[]{:S(2)}) collective-permute-start(f32[64,512]{1,0:T(8,128)S(1)} %get-tuple-element.14), channel_id=1, source_target_pairs={{0,1},{2,3},{4,5},{6,7},{8,9},{10,11},{12,13},{14,15},{16,17},{18,... | collective-permute-start | bytes 393224 | tf_op jit(solution)/shard_map/ppermute | solution.py:266
  47.4 60.1 %copy-start.15 = (f32[64,1024]{1,0:T(8,128)}, f32[64,1024]{1,0:T(8,128)S(1)}, u32[]{:S(2)}) copy-start(f32[64,1024]{1,0:T(8,128)S(1)} %get-tuple-element.31) | copy-start | bytes 786436
  47.4 8.5 %collective-permute-start.11 = (f32[64,1024]{1,0:T(8,128)S(1)}, f32[64,1024]{1,0:T(8,128)S(1)}, u32[]{:S(2)}, u32[]{:S(2)}) collective-permute-start(f32[64,1024]{1,0:T(8,128)S(1)} %get-tuple-element.25.refs_0_), channel_id=1, source_target_pairs={{8,0},{10,2},{12,4},{14,6},{16,8},{18,10},{20,12},{22,14},{24,16},... | collective-permute-start | bytes 786440 | tf_op jit(solution)/shard_map/ppermute | solution.py:266
  55.9 8.3 %collective-permute-start.13 = (f32[64,1024]{1,0:T(8,128)S(1)}, f32[64,1024]{1,0:T(8,128)S(1)}, u32[]{:S(2)}, u32[]{:S(2)}) collective-permute-start(f32[64,1024]{1,0:T(8,128)S(1)} %collective-permute-done.11.refs_2_), channel_id=1, source_target_pairs={{8,0},{10,2},{12,4},{14,6},{16,8},{18,10},{20,12},{22,14},{24,16},... | collective-permute-start | bytes 786440 | tf_op jit(solution)/shard_map/ppermute | solution.py:266
  64.2 6.4 %collective-permute-start.14 = (f32[64,1024]{1,0:T(8,128)S(1)}, f32[64,1024]{1,0:T(8,128)S(1)}, u32[]{:S(2)}, u32[]{:S(2)}) collective-permute-start(f32[64,1024]{1,0:T(8,128)S(1)} %get-tuple-element.36), channel_id=1, source_target_pairs={{0,4},{2,6},{4,0},{6,2},{8,12},{10,14},{12,8},{14,10},{16,20},{18,... | collective-permute-start | bytes 786440 | tf_op jit(solution)/shard_map/ppermute | solution.py:270
  65.8 7.7 %collective-permute-start.12 = (f32[64,1024]{1,0:T(8,128)S(1)}, f32[64,1024]{1,0:T(8,128)S(1)}, u32[]{:S(2)}, u32[]{:S(2)}) collective-permute-start(f32[64,1024]{1,0:T(8,128)S(1)} %get-tuple-element.37), channel_id=1, source_target_pairs={{0,4},{2,6},{4,0},{6,2},{8,12},{10,14},{12,8},{14,10},{16,20},{18,... | collective-permute-start | bytes 786440 | tf_op jit(solution)/shard_map/ppermute | solution.py:270
  74.7 32.8 %collective-permute-start.15 = (f32[4,64,1024]{2,1,0:T(8,128)}, f32[4,64,1024]{2,1,0:T(8,128)S(1)}, u32[]{:S(2)}, u32[]{:S(2)}) collective-permute-start(f32[4,64,1024]{2,1,0:T(8,128)} %pad_maximum_fusion), channel_id=1, source_target_pairs={{0,2},{2,0},{4,6},{6,4},{8,10},{10,8},{12,14},{14,12},{16,18},{18,... | collective-permute-start | bytes 3145736 | tf_op jit(solution)/shard_map/ppermute | solution.py:270
  76.6 1.4 %collective-permute-start.6 = (f32[1,128]{1,0:T(1,128)S(1)}, f32[1,128]{1,0:T(1,128)S(1)}, u32[]{:S(2)}, u32[]{:S(2)}) collective-permute-start(f32[1,128]{1,0:T(1,128)S(1)} %broadcast_in_dim.7), channel_id=1, source_target_pairs={{0,2},{2,0},{4,6},{6,4},{8,10},{10,8},{12,14},{14,12},{16,18},{18,... | collective-permute-start | bytes 1544 | tf_op jit(solution)/shard_map/ppermute | solution.py:270
  78.0 3.6 %collective-permute-start.7 = (f32[1,128]{1,0:T(1,128)S(1)}, f32[1,128]{1,0:T(1,128)S(1)}, u32[]{:S(2)}, u32[]{:S(2)}) collective-permute-start(f32[1,128]{1,0:T(1,128)S(1)} %broadcast_add_fusion), channel_id=1, source_target_pairs={{0,4},{2,6},{4,0},{6,2},{8,12},{10,14},{12,8},{14,10},{16,20},{18,... | collective-permute-start | bytes 1544 | tf_op jit(solution)/shard_map/ppermute | solution.py:270
  81.6 3.6 %collective-permute-start.8 = (f32[1,128]{1,0:T(1,128)S(1)}, f32[1,128]{1,0:T(1,128)S(1)}, u32[]{:S(2)}, u32[]{:S(2)}) collective-permute-start(f32[1,128]{1,0:T(1,128)S(1)} %fusion.16), channel_id=1, source_target_pairs={{0,8},{2,10},{4,12},{6,14},{8,0},{10,2},{12,4},{14,6},{16,24},{18,... | collective-permute-start | bytes 1544 | tf_op jit(solution)/shard_map/ppermute | solution.py:270
  85.2 4.5 %collective-permute-start.9 = (f32[1,128]{1,0:T(1,128)S(1)}, f32[1,128]{1,0:T(1,128)S(1)}, u32[]{:S(2)}, u32[]{:S(2)}) collective-permute-start(f32[1,128]{1,0:T(1,128)S(1)} %add.114), channel_id=1, source_target_pairs={{0,16},{2,18},{4,20},{6,22},{8,24},{10,26},{12,28},{14,30},{16,0},... | collective-permute-start | bytes 1544 | tf_op jit(solution)/shard_map/ppermute | solution.py:270
  89.6 5.3 %collective-permute-start.10 = (f32[1,128]{1,0:T(1,128)S(1)}, f32[1,128]{1,0:T(1,128)S(1)}, u32[]{:S(2)}, u32[]{:S(2)}) collective-permute-start(f32[1,128]{1,0:T(1,128)S(1)} %add.115), channel_id=1, source_target_pairs={{0,1},{1,0},{2,3},{3,2},{4,5},{5,4},{6,7},{7,6},{8,9},{9,8},{10,11... | collective-permute-start | bytes 1544 | tf_op jit(solution)/shard_map/ppermute | solution.py:270
  93.7 6.9 %collective-permute-start.16 = (f32[64,512]{1,0:T(8,128)S(1)}, f32[64,512]{1,0:T(8,128)S(1)}, u32[]{:S(2)}, u32[]{:S(2)}) collective-permute-start(f32[64,512]{1,0:T(8,128)S(1)} %slice.69), channel_id=1, source_target_pairs={{1,0},{3,2},{5,4},{7,6},{9,8},{11,10},{13,12},{15,14},{17,16},{19,... | collective-permute-start | bytes 393224 | tf_op jit(solution)/shard_map/ppermute | solution.py:266
  103.2 5.3 %copy-start.2 = (f32[8,64,1024]{2,1,0:T(8,128)S(1)}, f32[8,64,1024]{2,1,0:T(8,128)}, u32[]{:S(2)}) copy-start(f32[8,64,1024]{2,1,0:T(8,128)} %refs_8_.1) | copy-start | bytes 6291460
  103.2 5.3 %copy-start.7 = (s32[64,1024]{1,0:T(8,128)S(1)}, s32[64,1024]{1,0:T(8,128)}, u32[]{:S(2)}) copy-start(s32[64,1024]{1,0:T(8,128)} %refs_7_.1) | copy-start | bytes 786436
  103.2 5.3 %copy-start.10 = (f32[8,512]{1,0:T(8,128)S(1)}, f32[8,512]{1,0:T(8,128)}, u32[]{:S(2)}) copy-start(f32[8,512]{1,0:T(8,128)} %profile_ref.5) | copy-start | bytes 49156
  116.7 11.0 %all-to-all-start = ((f32[32,1,128]{2,1,0:T(1,128)}), f32[32,1,128]{2,1,0:T(1,128)S(1)}, u32[]{:S(2)}, u32[]{:S(2)}) async-start(f32[32,1,128]{2,1,0:T(1,128)} %broadcast_in_dim.8), calls=%async_computation | async-start | bytes 32768 | tf_op jit(solution)/shard_map/all_to_all | solution.py:287
  (8 other events, 9.7 us)
